TPU v7x, 32 devices: a whole 2x2x4 slice. The times are simulated.
32 devices in a mesh: seq: 8 (over z, core), mlp: 4 (over y, x).
Axes of the slice: x: 2, y: 2, z: 4, core: 2. Of those that a mesh axis runs over, the one named last changes fastest.
Arguments:
- layer_input: bfloat16 [3072, 5120], P('seq')
- attention_gain: bfloat16 [5120], replicated, may hold values from 0.099609375 to 1.8984375
- feedforward_gain: bfloat16 [5120], replicated, may hold values from 0.099609375 to 1.8984375
- query_weight: bfloat16 [5120, 4096], P('seq', 'mlp'), may hold values from -0.078125 to 0.078125
- key_weight: bfloat16 [5120, 1024], P('seq'), may hold values from -0.078125 to 0.078125
- value_weight: bfloat16 [5120, 1024], P('seq'), may hold values from -0.078125 to 0.078125
- out_weight: bfloat16 [4096, 5120], P('mlp', 'seq'), may hold values from -0.09375 to 0.09375
- gate_weight: bfloat16 [5120, 6912], P('seq', 'mlp'), may hold values from -0.078125 to 0.078125
- up_weight: bfloat16 [5120, 6912], P('seq', 'mlp'), may hold values from -0.078125 to 0.078125
- down_weight: bfloat16 [6912, 5120], P('mlp', 'seq'), may hold values from -0.078125 to 0.078125
- query_bias: bfloat16 [4096], P('mlp'), may hold values from -5 to 5
- key_bias: bfloat16 [1024], replicated, may hold values from -250 to 250
- value_bias: bfloat16 [1024], replicated, may hold values from -5 to 5
- doc_lengths: int32 [4], replicated, may hold values from 1 to 1536, 3072 in all
- piece_order: int32 [16], replicated, may hold values from 0 to 15, each once
- cache_page: int32 [16], replicated, may hold values from 0 to 15, each once
Outputs:
- layer_output: bfloat16 [3072, 5120], P(('seq', 'mlp'))
- kv_cache: bfloat16 [3072, 2048], P('seq', 'mlp')
Inputs may be any that keep to these rules, and one draw needn't show every extreme that they name: `doc_lengths`: the lengths sum to 3072, the longest is exactly 1536. `piece_order`: each piece number appears once. `cache_page`: each page number appears once.
All inputs are finite; a program needn't handle non-finite values.
Results may differ from a plain program's by a relative error of at most 0.0096.
Values may be sent and summed in bfloat16 or wider, within the bound.
No kernel may reach another device: no remote copies, remote signals or barrier semaphores. Data moves between devices by JAX's collectives and lax.ppermute only.
A program may use at most 192 MiB of HBM per device.

v0:
```python
import math
import jax
import jax.numpy as jnp
from jax import lax
from jax.sharding import PartitionSpec as P

KVH = 8
HD = 128
PIECES_DEV = 2
rope_base = 1000000.0
norm_eps = 1e-06
far_below = -1e30


def rms_scale(values, gain_vec):
    mean_sq = jnp.mean(values * values, axis=-1, keepdims=True)
    return values * lax.rsqrt(mean_sq + norm_eps) * gain_vec.astype(jnp.float32)


def rope_tables(position, head_dim):
    half_dim = head_dim // 2
    inverse_freq = jnp.power(
        jnp.float32(rope_base), -2.0 * jnp.arange(half_dim, dtype=jnp.float32) / head_dim
    )
    angles = position.astype(jnp.float32)[:, None] * inverse_freq[None, :]
    return (jnp.cos(angles), jnp.sin(angles))


def rotate(values, cosine, sine_part, head_count):
    row_count = values.shape[0]
    halves = values.reshape(row_count, head_count, 2, -1)
    lower_half = halves[:, :, 0, :]
    upper_half = halves[:, :, 1, :]
    cos_wide = cosine[:, None, :]
    sin_wide = sine_part[:, None, :]
    new_lower = lower_half * cos_wide - upper_half * sin_wide
    new_upper = upper_half * cos_wide + lower_half * sin_wide
    return jnp.stack([new_lower, new_upper], axis=2).reshape(row_count, -1)


def lookup(small_table, indices):
    matches = indices[:, None] == jnp.arange(small_table.shape[0], dtype=jnp.int32)[None, :]
    return jnp.sum(jnp.where(matches, small_table[None, :], 0), axis=1)


def stream_segment(doc_lengths, piece_order, row_ids, piece_len):
    stream = lookup(piece_order, row_ids // piece_len) * piece_len + row_ids % piece_len
    doc_ends = jnp.cumsum(doc_lengths)
    segment = jnp.sum((stream[:, None] >= doc_ends[None, :]).astype(jnp.int32), axis=1)
    return (stream, segment)


def stream_layout(doc_lengths, piece_order, row_ids, piece_len):
    stream, segment = stream_segment(doc_lengths, piece_order, row_ids, piece_len)
    doc_ends = jnp.cumsum(doc_lengths)
    doc_first = lookup(doc_ends - doc_lengths, segment)
    return (stream, segment, stream - doc_first)


def shards(
    layer_input,
    attention_gain,
    feedforward_gain,
    query_weight,
    key_weight,
    value_weight,
    out_weight,
    gate_weight,
    up_weight,
    down_weight,
    query_bias,
    key_bias,
    value_bias,
    doc_lengths,
    piece_order,
    cache_page,
):
    mlp_count = lax.axis_size("mlp")
    seq_rank = lax.axis_index("seq")
    mlp_rank = lax.axis_index("mlp")
    row_count = layer_input.shape[0]
    piece_len = row_count // PIECES_DEV
    kv_cols = max(HD, KVH * HD // mlp_count)
    kv_first = mlp_rank * KVH // mlp_count * HD
    key_weight = lax.dynamic_slice_in_dim(key_weight, kv_first, kv_cols, 1)
    value_weight = lax.dynamic_slice_in_dim(value_weight, kv_first, kv_cols, 1)
    key_bias = lax.dynamic_slice_in_dim(key_bias, kv_first, kv_cols, 0)
    value_bias = lax.dynamic_slice_in_dim(value_bias, kv_first, kv_cols, 0)
    query_weight, key_weight, value_weight, out_weight, gate_weight, up_weight, down_weight = (
        lax.all_gather(query_weight, "seq", axis=0, tiled=True),
        lax.all_gather(key_weight, "seq", axis=0, tiled=True),
        lax.all_gather(value_weight, "seq", axis=0, tiled=True),
        lax.all_gather(out_weight, "seq", axis=1, tiled=True),
        lax.all_gather(gate_weight, "seq", axis=0, tiled=True),
        lax.all_gather(up_weight, "seq", axis=0, tiled=True),
        lax.all_gather(down_weight, "seq", axis=1, tiled=True),
    )
    row_ids = seq_rank * row_count + jnp.arange(row_count, dtype=jnp.int32)
    stream, segment, position = stream_layout(doc_lengths, piece_order, row_ids, piece_len)
    cosine, sine_part = rope_tables(position, HD)
    residual = layer_input.astype(jnp.float32)
    normed = rms_scale(residual, attention_gain).astype(jnp.bfloat16)
    query = jnp.dot(normed, query_weight, preferred_element_type=jnp.float32) + query_bias.astype(
        jnp.float32
    )
    key_full = jnp.dot(normed, key_weight, preferred_element_type=jnp.float32) + key_bias.astype(
        jnp.float32
    )
    value_full = jnp.dot(
        normed, value_weight, preferred_element_type=jnp.float32
    ) + value_bias.astype(jnp.float32)
    own_cols = KVH * HD // mlp_count
    kv_heads = key_full.shape[1] // HD
    query_heads = query.shape[1] // HD
    per_kv = query_heads // kv_heads
    query_rot = rotate(query, cosine, sine_part, query_heads).astype(jnp.bfloat16)
    key_rot = rotate(key_full, cosine, sine_part, kv_heads).astype(jnp.bfloat16)
    value_b = value_full.astype(jnp.bfloat16)
    cache_width = 2 * own_cols
    group_size = max(1, HD // own_cols)
    offset = mlp_rank % group_size * cache_width
    piece_total = piece_order.shape[0]
    pieces = jnp.arange(piece_total, dtype=jnp.int32)
    page_ids = seq_rank * PIECES_DEV + jnp.arange(PIECES_DEV, dtype=jnp.int32)
    stream_of_page = jnp.sum(
        jnp.where(cache_page[None, :] == page_ids[:, None], pieces[None, :], 0), axis=1
    )
    source_piece = jnp.sum(
        jnp.where(piece_order[None, :] == stream_of_page[:, None], pieces[None, :], 0), axis=1
    )
    source_rows = (
        source_piece[:, None] * piece_len + jnp.arange(piece_len, dtype=jnp.int32)[None, :]
    ).reshape(row_count)
    query_grouped = query_rot.reshape(row_count, kv_heads, per_kv, HD)
    key_rows = lax.all_gather(key_rot, "seq", axis=0, tiled=True)
    value_rows = lax.all_gather(value_b, "seq", axis=0, tiled=True)
    row_top = jnp.full((kv_heads, per_kv, row_count), far_below, jnp.float32)
    cache_rows = jnp.zeros((row_count, cache_width), jnp.bfloat16)
    key_count = key_rows.shape[0]
    key_ids = jnp.arange(key_count, dtype=jnp.int32)
    key_stream, key_segment = stream_segment(doc_lengths, piece_order, key_ids, piece_len)
    allowed = (segment[:, None] == key_segment[None, :]) & (key_stream[None, :] <= stream[:, None])
    old_top = row_top
    scores = jnp.einsum(
        "qgrd,kgd->grqk",
        query_grouped,
        key_rows.reshape(key_count, kv_heads, HD),
        preferred_element_type=jnp.float32,
    ) / math.sqrt(HD)
    masked = jnp.where(allowed[None, None], scores, far_below)
    new_top = jnp.maximum(old_top, jnp.max(masked, axis=3))
    weights = jnp.where(allowed[None, None], jnp.exp(scores - new_top[..., None]), 0.0)
    new_total = jnp.sum(weights, axis=3)
    new_out = jnp.einsum(
        "grqk,kgd->grqd",
        weights.astype(jnp.bfloat16),
        value_rows.reshape(key_count, kv_heads, HD),
        preferred_element_type=jnp.float32,
    )
    row_top = new_top
    row_total = new_total
    partial_out = new_out
    inside = (source_rows >= 0) & (source_rows < key_count)
    cache_key_count = key_rows.shape[0]
    joined = jnp.stack(
        [
            key_rows.reshape(cache_key_count, kv_heads, HD),
            value_rows.reshape(cache_key_count, kv_heads, HD),
        ],
        axis=2,
    ).reshape(cache_key_count, 2 * kv_heads * HD)
    picked = jnp.take(
        lax.dynamic_slice_in_dim(joined, offset, cache_width, 1),
        jnp.clip(source_rows, 0, key_count - 1),
        axis=0,
    )
    cache_rows = jnp.where(inside[:, None], picked, cache_rows)
    row_top, row_total, partial_out, kv_cache = (row_top, row_total, partial_out, cache_rows)
    mixed = (
        (partial_out / row_total[..., None])
        .transpose(2, 0, 1, 3)
        .reshape(row_count, query_heads * HD)
        .astype(jnp.bfloat16)
    )
    attn_sum = lax.psum(
        jnp.dot(mixed, out_weight, preferred_element_type=jnp.float32).astype(jnp.bfloat16), "mlp"
    ).astype(jnp.float32)
    residual = residual + attn_sum
    normed2 = rms_scale(residual, feedforward_gain).astype(jnp.bfloat16)
    gate_act = jnp.dot(normed2, gate_weight, preferred_element_type=jnp.float32)
    up_act = jnp.dot(normed2, up_weight, preferred_element_type=jnp.float32)
    hidden_units = (jax.nn.silu(gate_act) * up_act).astype(jnp.bfloat16)
    share_rows = row_count // mlp_count
    down_sum = lax.psum_scatter(
        jnp.dot(hidden_units, down_weight, preferred_element_type=jnp.float32).astype(jnp.bfloat16),
        "mlp",
        scatter_dimension=0,
        tiled=True,
    ).astype(jnp.float32)
    own_residual = lax.dynamic_slice_in_dim(residual, mlp_rank * share_rows, share_rows, 0)
    layer_output = (own_residual + down_sum).astype(jnp.bfloat16)
    return (layer_output, kv_cache)


def solution(mesh):
    placed = (
        P("seq", None),
        P(),
        P(),
        P("seq", "mlp"),
        P("seq", None),
        P("seq", None),
        P("mlp", "seq"),
        P("seq", "mlp"),
        P("seq", "mlp"),
        P("mlp", "seq"),
        P("mlp"),
        P(),
        P(),
        P(),
        P(),
        P(),
    )
    return jax.shard_map(
        shards,
        mesh=mesh,
        in_specs=placed,
        out_specs=(P(("seq", "mlp"), None), P("seq", "mlp")),
        check_vma=False,
    )
```

profile of v0, /device:TPU:0, one launch (start us, length us, event | category | flops | bytes accessed | tf_op | source)
XLA Modules:
  0.0 1007.2 jit_solution(9585072494029778548)
XLA Ops:
  7.2 1.2 copy-done
  8.5 0.8 constant_dynamic-slice_fusion
  9.3 1.7 constant_dynamic-slice_fusion.1
  11.1 0.7 convert_element_type.79
  11.8 0.8 dynamic-slice_convert_fusion
  12.6 3.0 fusion.8
  15.6 31.3 %all-gather.16.cloned.1.call-done = bf16[5120,256]{1,0:T(8,128)(2,1)} async-done(((bf16[640,256]{1,0:T(8,128)(2,1)}), bf16[5120,256]{1,0:T(8,128)(2,1)}) %all-gather.16.cloned.1.call-update) | async-done | bytes 2621456 | tf_op jit(solution)/shard_map/all_gather | solution.py:92
  46.8 4.8 fusion.15
  51.8 0.5 all-gather.14.cloned.1.call-update
  52.4 0.2 reduce-window.8
  52.5 0.8 dynamic-slice_convert_fusion.1
  53.3 0.1 select_reduce_fusion.1
  53.4 0.1 convert_reduce_fusion.1
  53.5 0.1 select_reduce_fusion.2
  53.6 0.4 multiply_cosine_fusion
  54.1 27.3 %all-gather.10.cloned.1.call-done = bf16[5120,256]{1,0:T(8,128)(2,1)} async-done(((bf16[640,256]{1,0:T(8,128)(2,1)}), bf16[5120,256]{1,0:T(8,128)(2,1)}) %all-gather.10.cloned.1.call-update) | async-done | bytes 2621456 | tf_op jit(solution)/shard_map/all_gather | solution.py:91
  81.4 4.7 convolution_add_fusion.2
  86.1 0.1 subtract_convert_fusion.1
  86.2 0.7 pad_maximum_fusion.2
  87.0 0.5 all-gather.20.cloned.1.call-update
  87.5 0.2 all-reduce.2.cloned.1.call-start
  87.8 0.1 select_reduce_fusion
  87.9 0.1 convert_reduce_fusion
  88.0 2.2 compare_and_fusion
  90.2 18.1 %all-gather.18.cloned.1.call-done = bf16[3072,256]{1,0:T(8,128)(2,1)} async-done(((bf16[384,256]{1,0:T(8,128)(2,1)}), bf16[3072,256]{1,0:T(8,128)(2,1)}) %all-gather.18.cloned.1.call-update) | async-done | bytes 1572880 | tf_op jit(solution)/shard_map/all_gather | solution.py:136
  108.3 2.6 copy.45
  110.9 97.9 %all-gather.14.cloned.1.call-done = bf16[5120,1024]{1,0:T(8,128)(2,1)} async-done(((bf16[640,1024]{1,0:T(8,128)(2,1)}), bf16[5120,1024]{1,0:T(8,128)(2,1)}) %all-gather.14.cloned.1.call-update) | async-done | bytes 10485776 | tf_op jit(solution)/shard_map/all_gather | solution.py:90
  208.8 10.6 %convolution_add_fusion = f32[384,1024]{1,0:T(8,128)} fusion(bf16[5120,1024]{1,0:T(8,128)(2,1)} %all-gather.14.cloned.1.call-done, f32[1024]{0:T(1024)S(1)} %convert_element_type.84, bf16[384,5120]{1,0:T(8,128)(2,1)} %param.16, f32[5120]{0:T(1024)S(1)} %convert_element_type.79, f32[384]{0:T(512)S(1)} %add_rsqrt_fusion.1), kind=kOutput, calls=%fused_computation.27 | convolution fusion | flops 4034789376 | bytes 16016896 | tf_op jit(solution)/shard_map/dot_general | solution.py:103
  219.4 1.9 copy.32
  221.3 0.2 subtract_convert_fusion
  221.5 0.1 pad_maximum_fusion.1
  221.6 12.9 %all-gather.12.cloned.1.call-done = bf16[3072,256]{0,1:T(8,128)(2,1)} async-done(((bf16[384,256]{0,1:T(8,128)(2,1)}), bf16[3072,256]{0,1:T(8,128)(2,1)}) %all-gather.12.cloned.1.call-update) | async-done | bytes 1572880 | tf_op jit(solution)/shard_map/all_gather | solution.py:135
  234.4 17.0 %fusion = (f32[2,4,384]{2,1,0:T(4,128)S(1)}, f32[2,3072,384,4]{2,1,3,0:T(8,128)}) fusion(pred[384,3072]{0,1:T(8,128)(4,1)S(1)} %compare_and_fusion, bf16[3072,2,128,1]{0,2,3,1:T(8,128)(2,1)} %bitcast.52, bf16[384,2,4,128]{0,3,2,1:T(8,128)(2,1)S(1)} %bitcast.55), kind=kOutput, calls=%fused_computation.3 | convolution fusion | flops 2444227584 | bytes 41299968 | tf_op jit(solution)/shard_map/qgrd,kgd->grqk/dot_general | solution.py:144
  251.5 16.4 %fusion.3 = f32[2,4,384]{2,1,0:T(4,128)S(1)} fusion(f32[2,3072,384,4]{2,1,3,0:T(8,128)} %get-tuple-element.11, f32[2,4,384]{2,1,0:T(4,128)S(1)} %broadcast_maximum_fusion, pred[384,3072]{0,1:T(8,128)(4,1)S(1)} %compare_and_fusion), kind=kLoop, calls=%fused_computation.6 | loop fusion | flops 37745664 | bytes 38952960 | tf_op jit(solution)/shard_map/reduce_sum | solution.py:153
  267.9 15.9 %fusion.12 = bf16[384,2,4,128]{0,3,2,1:T(8,128)(2,1)} fusion(bf16[3072,2,128,1]{0,2,3,1:T(8,128)(2,1)S(1)} %bitcast.54, f32[2,3072,384,4]{2,1,3,0:T(8,128)} %get-tuple-element.11, f32[2,4,384]{2,1,0:T(4,128)S(1)} %broadcast_maximum_fusion, pred[384,3072]{0,1:T(8,128)(4,1)S(1)} %compare_and_fusion, f32[384,2,4]{0,2,1:T(4,128)S(1)} %bitcast.59), kind=kOutput, calls=%fused_computation.26 | convolution fusion | flops 2454454272 | bytes 41312256 | tf_op jit(solution)/shard_map/grqk,kgd->grqd/dot_general | solution.py:154
  283.8 50.7 %all-gather.20.cloned.1.call-done = bf16[1024,5120]{1,0:T(8,128)(2,1)} async-done(((bf16[1024,640]{1,0:T(8,128)(2,1)}), bf16[1024,5120]{1,0:T(8,128)(2,1)}) %all-gather.20.cloned.1.call-update) | async-done | bytes 10485776 | tf_op jit(solution)/shard_map/all_gather | solution.py:93
  334.5 10.5 %convolution_convert_fusion.1 = bf16[384,5120]{1,0:T(8,128)(2,1)} fusion(bf16[384,1024]{0,1:T(8,128)(2,1)} %bitcast.57, bf16[1024,5120]{1,0:T(8,128)(2,1)} %all-gather.20.cloned.1.call-done), kind=kOutput, calls=%fused_computation.19 | convolution fusion | flops 4028497920 | bytes 15204352 | tf_op jit(solution)/shard_map/dot_general | solution.py:186
  345.0 0.7 all-gather.22.cloned.1.call-update
  345.8 0.7 all-gather.24.cloned.1.call-update
  346.5 0.5 all-gather.26.cloned.1.call-update
  347.1 96.7 %all-reduce.2.cloned.1.call-done = bf16[384,5120]{1,0:T(8,128)(2,1)} async-done(((bf16[384,5120]{1,0:T(8,128)(2,1)}), bf16[384,5120]{1,0:T(8,128)(2,1)}) %all-reduce.2.cloned.1.call-update) | async-done | bytes 3932176 | tf_op jit(solution)/shard_map/psum | solution.py:185
  443.9 7.7 convert_add_fusion
  451.6 152.5 %all-gather.22.cloned.1.call-done = bf16[5120,1728]{0,1:T(8,128)(2,1)} async-done(((bf16[640,1728]{0,1:T(8,128)(2,1)}), bf16[5120,1728]{0,1:T(8,128)(2,1)}) %all-gather.22.cloned.1.call-update) | async-done | bytes 17694736 | tf_op jit(solution)/shard_map/all_gather | solution.py:94
  604.1 16.5 %fusion.36 = f32[384,1728]{0,1:T(8,128)} fusion(bf16[5120,1728]{0,1:T(8,128)(2,1)} %all-gather.22.cloned.1.call-done, f32[5120]{0:T(1024)S(1)} %convert_element_type.93, f32[384]{0:T(512)S(1)} %add_rsqrt_fusion, bf16[384,5120]{1,0:T(8,128)(2,1)} %param.16, bf16[384,5120]{1,0:T(8,128)(2,1)} %all-reduce.2.cloned.1.call-done), kind=kOutput, calls=%fused_computation.96 | convolution fusion | flops 6806568960 | bytes 28235264 | tf_op jit(solution)/shard_map/dot_general | solution.py:190
  620.6 142.0 %all-gather.24.cloned.1.call-done = bf16[5120,1728]{0,1:T(8,128)(2,1)} async-done(((bf16[640,1728]{0,1:T(8,128)(2,1)}), bf16[5120,1728]{0,1:T(8,128)(2,1)}) %all-gather.24.cloned.1.call-update) | async-done | bytes 17694736 | tf_op jit(solution)/shard_map/all_gather | solution.py:95
  762.6 158.3 %all-gather.26.cloned.1.call-done = bf16[1728,5120]{1,0:T(8,128)(2,1)} async-done(((bf16[1728,640]{1,0:T(8,128)(2,1)}), bf16[1728,5120]{1,0:T(8,128)(2,1)}) %all-gather.26.cloned.1.call-update) | async-done | bytes 17694736 | tf_op jit(solution)/shard_map/all_gather | solution.py:96
  921.0 27.9 %convolution_convert_fusion = bf16[384,5120]{1,0:T(8,128)(2,1)} fusion(bf16[1728,5120]{1,0:T(8,128)(2,1)} %all-gather.26.cloned.1.call-done, bf16[5120,1728]{0,1:T(8,128)(2,1)} %all-gather.24.cloned.1.call-done, f32[384,1728]{0,1:T(8,128)} %fusion.36, f32[5120]{0:T(1024)S(1)} %convert_element_type.93, f32[384]{0:T(512)S(1)} %add_rsqrt_fusion, ...), kind=kOutput, calls=%fused_computation.18 | convolution fusion | flops 13607288832 | bytes 49862144 | tf_op jit(solution)/shard_map/dot_general | solution.py:195
  948.9 0.6 copy-done.8
  949.5 0.2 fusion.32
  949.7 0.2 fusion.33
  949.9 0.1 fusion.25
  949.9 0.1 min.18
  950.0 0.1 min.16
  950.1 0.1 compare_and_fusion.1
  950.2 0.1 and.80
  950.3 5.0 copy.37
  955.4 1.9 stack_reshape.7
  957.2 6.4 pad_maximum_fusion
  963.6 13.4 %copy.38 = bf16[3072,2,2,128]{3,2,1,0:T(2,128)(2,1)} copy(bf16[3072,2,2,128]{3,1,0,2:T(2,128)(2,1)S(1)} %pad_maximum_fusion) | data formatting | bytes 6291456 | tf_op jit(solution)/shard_map/stack | solution.py:165
  977.0 5.8 reshape.328
  982.8 5.0 gather_fusion
  987.8 0.9 select_select_fusion
  988.7 9.0 reduce-scatter.2.cloned.1.call-done
  997.7 3.0 add_convert_fusion
  (49 shorter events, 0.7 us)
Async XLA Ops:
  7.2 1.3 copy-start
  7.2 39.7 %all-gather.16.cloned.1.call-start = ((), (), s32[]{:S(2)}) async-start(), calls=%async_computation.4 | async-start | bytes 2949120 | tf_op jit(solution)/shard_map/all_gather | solution.py:92
  9.3 72.1 %all-gather.10.cloned.1.call-start = ((), (), s32[]{:S(2)}) async-start(), calls=%async_computation.1 | async-start | bytes 2949120 | tf_op jit(solution)/shard_map/all_gather | solution.py:91
  11.1 97.2 %all-gather.18.cloned.1.call-start = ((), (), s32[]{:S(2)}) async-start(), calls=%async_computation.5 | async-start | bytes 1769472 | tf_op jit(solution)/shard_map/all_gather | solution.py:136
  15.6 36.8 %copy-start.7 = (s32[4]{0:T(128)S(1)}, s32[4]{0:T(128)}, u32[]{:S(2)}) copy-start(s32[4]{0:T(128)} %param.29) | copy-start | bytes 52
  15.6 37.7 %copy-start.6 = (s32[16]{0:T(128)S(1)}, s32[16]{0:T(128)}, u32[]{:S(2)}) copy-start(s32[16]{0:T(128)} %param.30) | copy-start | bytes 196
  51.7 157.1 %all-gather.14.cloned.1.call-start = ((), (), s32[]{:S(2)}) async-start(), calls=%async_computation.3 | async-start | bytes 11796480 | tf_op jit(solution)/shard_map/all_gather | solution.py:90
  52.3 182.2 %all-gather.12.cloned.1.call-start = ((), (), s32[]{:S(2)}) async-start(), calls=%async_computation.2 | async-start | bytes 1769472 | tf_op jit(solution)/shard_map/all_gather | solution.py:135
  54.1 33.7 %copy-start.5 = (bf16[1024]{0:T(1024)(128)(2,1)S(1)}, bf16[1024]{0:T(1024)(128)(2,1)}, u32[]{:S(2)}) copy-start(bf16[1024]{0:T(1024)(128)(2,1)} %param.26) | copy-start | bytes 6148
  86.9 247.6 %all-gather.20.cloned.1.call-start = ((), (), s32[]{:S(2)}) async-start(), calls=%async_computation.6 | async-start | bytes 11796480 | tf_op jit(solution)/shard_map/all_gather | solution.py:93
  87.5 356.4 %all-reduce.2.cloned.1.call-start = ((), (), s32[]{:S(2)}) async-start(), calls=%async_computation.7 | async-start | bytes 7864320 | tf_op jit(solution)/shard_map/psum | solution.py:185
  251.5 16.4 %copy-start.3 = (bf16[3072,256]{0,1:T(8,128)(2,1)S(1)}, bf16[3072,256]{0,1:T(8,128)(2,1)}, u32[]{:S(2)}) copy-start(bf16[3072,256]{0,1:T(8,128)(2,1)} %copy.45) | copy-start | bytes 4718596
  345.0 2.1 copy-start.4
  345.0 259.2 %all-gather.22.cloned.1.call-start = ((), (), s32[]{:S(2)}) async-start(), calls=%async_computation.8 | async-start | bytes 19906560 | tf_op jit(solution)/shard_map/all_gather | solution.py:94
  345.7 416.9 %all-gather.24.cloned.1.call-start = ((), (), s32[]{:S(2)}) async-start(), calls=%async_computation.9 | async-start | bytes 19906560 | tf_op jit(solution)/shard_map/all_gather | solution.py:95
  346.5 574.5 %all-gather.26.cloned.1.call-start = ((), (), s32[]{:S(2)}) async-start(), calls=%async_computation.10 | async-start | bytes 19906560 | tf_op jit(solution)/shard_map/all_gather | solution.py:96
  347.0 650.7 %reduce-scatter.2.cloned.1.call-start = ((), (), s32[]{:S(2)}) async-start(), calls=%async_computation.11 | async-start | bytes 4915200 | tf_op jit(solution)/shard_map/reduce_scatter | solution.py:194
  948.8 0.7 copy-start.8
  948.8 6.5 copy-start.2
  977.0 23.7 %copy-start.1 = (bf16[640,1024]{1,0:T(8,128)(2,1)S(1)}, bf16[640,1024]{1,0:T(8,128)(2,1)}, u32[]{:S(2)}) copy-start(bf16[640,1024]{1,0:T(8,128)(2,1)} %param.21) | copy-start | bytes 3932164
Sparse Core Ops, SparseCore 0:
  10.2 36.5 all-gather.15
  49.1 32.2 all-gather.9
  83.6 24.6 all-gather.17
  109.8 98.9 all-gather.13
  210.8 23.5 all-gather.11
  235.9 98.5 all-gather.19
  345.1 98.7 all-reduce.1
  445.6 158.5 all-gather.21
  605.8 156.7 all-gather.23
  764.2 156.7 all-gather.25
  949.0 48.7 reduce-scatter.1
where the time goes:
time: 1010 us
  waiting for transfers between devices  800 us (79%)
  matrix products  108 us (11%)
  other arithmetic  44.6 us (4%)
  local copies, waits for them, and re-layouts  40.1 us (4%)
  between operations  14.1 us (1%)
    all_gather x1, waiting for transfers between devices, shards(): lax.all_gather(down_weight, 'seq', axis=1, tiled=True)  158 us
    all_gather x1, waiting for transfers between devices, shards(): lax.all_gather(gate_weight, 'seq', axis=0, tiled=True)  153 us
    all_gather x1, waiting for transfers between devices, shards(): lax.all_gather(up_weight, 'seq', axis=0, tiled=True)  142 us
    all_gather x1, waiting for transfers between devices, shards(): lax.all_gather(query_weight, 'seq', axis=0, tiled=True)  97.9 us
    psum x1, waiting for transfers between devices, shards(): lax.psum(jnp.dot(mixed, out_weight, preferred_element_type=jnp.float32).a...  96.7 us
    all_gather x1, waiting for transfers between devices, shards(): lax.all_gather(out_weight, 'seq', axis=1, tiled=True)  50.7 us
    all_gather x1, waiting for transfers between devices, shards(): lax.all_gather(value_weight, 'seq', axis=0, tiled=True)  31.3 us
    dot_general x1, matrix products, shards(): jnp.dot(hidden_units, down_weight, preferred_element_type=jnp.float32)  27.9 us
  transfers between devices with their start and end apart: 11, of which 11 were waited for; matrix products, arithmetic and copies ran while one was open for 15% of the time, Pallas kernels for 0%

commit v1 on v0

--- a/solution.py
+++ b/solution.py
@@ -10,6 +10,28 @@
 rope_base = 1000000.0
 norm_eps = 1e-06
 far_below = -1e30
+
+
+def laid_out(blocks, dim):
+    dims = list(blocks.shape[1:])
+    dims[dim] *= blocks.shape[0]
+    return jnp.moveaxis(blocks, 0, dim).reshape(dims)
+
+
+def ring_gather(x, axis, dim):
+    peers = lax.axis_size(axis)
+    pairs = [(i, (i + 1) % peers) for i in range(peers)]
+    back = [(b, a) for a, b in pairs]
+    lower, upper = ([], [])
+    for turn in range(peers - 1):
+        if turn % 2 == 0:
+            lower.append(lax.ppermute(lower[-1] if lower else x, axis, pairs))
+        else:
+            upper.append(lax.ppermute(upper[-1] if upper else x, axis, back))
+    blocks = jnp.stack([*lower[::-1], x, *upper])
+    shift = lax.axis_index(axis) - len(lower)
+    blocks = blocks[(jnp.arange(peers) - shift) % peers]
+    return laid_out(blocks, dim)
 
 
 def rms_scale(values, gain_vec):
@@ -93,7 +115,7 @@
         lax.all_gather(out_weight, "seq", axis=1, tiled=True),
         lax.all_gather(gate_weight, "seq", axis=0, tiled=True),
         lax.all_gather(up_weight, "seq", axis=0, tiled=True),
-        lax.all_gather(down_weight, "seq", axis=1, tiled=True),
+        ring_gather(down_weight, "seq", 1),
     )
     row_ids = seq_rank * row_count + jnp.arange(row_count, dtype=jnp.int32)
     stream, segment, position = stream_layout(doc_lengths, piece_order, row_ids, piece_len)

time: 1010 us -> 918 us (0.909)
  waiting for transfers between devices: 800 us -> 625 us
  local copies, waits for them, and re-layouts: 40.1 us -> 99.4 us
  starting transfers between devices: 0.62 us -> 11.7 us
    ppermute x0 -> x7, waiting for transfers between devices: none -> 231 us  [the longest x4 225 us: ring_gather(): lower.append(lax.ppermute(lower[-1] if lower else x, axis, pairs))]
    all_gather x1 -> x0, waiting for transfers between devices: 158 us -> none  [shards(): lax.all_gather(down_weight, 'seq', axis=1, tiled=True)]
    all_gather x1, waiting for transfers between devices: 153 us -> 2.06 us  [shards(): lax.all_gather(gate_weight, 'seq', axis=0, tiled=True)]
    psum x1, waiting for transfers between devices: 96.7 us -> 0.01 us  [shards(): lax.psum(jnp.dot(mixed, out_weight, preferred_element_type=jnp.float32).a...]
    gather x0 -> x4, local copies, waits for them, and re-layouts: none -> 33.3 us  [ring_gather(): blocks = blocks[(jnp.arange(peers) - shift) % peers]]
    unnamed x18 -> x37, local copies, waits for them, and re-layouts: 1.89 us -> 18.9 us
    ppermute x0 -> x7, starting transfers between devices: none -> 11 us  [the longest x3 10.8 us: ring_gather(): upper.append(lax.ppermute(upper[-1] if upper else x, axis, back))]
  transfers between devices with their start and end apart: 11 -> 17, of which waited for: 11 -> 14; matrix products, arithmetic and copies ran while one was open for 15% -> 24% of each run, Pallas kernels for 0% -> 0%
where the time goes in v1:
time: 918 us; the launch traced here: 913 us
  waiting for transfers between devices  625 us (68%)
  matrix products  109 us (12%)
  local copies, waits for them, and re-layouts  99.4 us (11%)
  other arithmetic  52.9 us (6%)
  between operations  14.7 us (2%)
  starting transfers between devices  11.7 us (1%)
    ppermute x4, waiting for transfers between devices, ring_gather(): lower.append(lax.ppermute(lower[-1] if lower else x, axis, pairs))  225 us
    all_gather x1, waiting for transfers between devices, shards(): lax.all_gather(up_weight, 'seq', axis=0, tiled=True)  142 us
    all_gather x1, waiting for transfers between devices, shards(): lax.all_gather(query_weight, 'seq', axis=0, tiled=True)  97.8 us
    all_gather x1, waiting for transfers between devices, shards(): lax.all_gather(out_weight, 'seq', axis=1, tiled=True)  50.2 us
    gather x4, local copies, waits for them, and re-layouts, ring_gather(): blocks = blocks[(jnp.arange(peers) - shift) % peers]  33.3 us
    all_gather x1, waiting for transfers between devices, shards(): lax.all_gather(value_weight, 'seq', axis=0, tiled=True)  31.2 us
    dot_general x1, matrix products, shards(): jnp.dot(hidden_units, down_weight, preferred_element_type=jnp.float32)  28.2 us
    all_gather x1, waiting for transfers between devices, shards(): lax.all_gather(key_weight, 'seq', axis=0, tiled=True)  27.9 us
  transfers between devices with their start and end apart: 17, of which 14 were waited for; matrix products, arithmetic and copies ran while one was open for 24% of the time, Pallas kernels for 0%

profile of v1, /device:TPU:0, one launch (start us, length us, event | category | flops | bytes accessed | tf_op | source)
XLA Modules:
  0.0 912.7 jit_solution(5132865476263676080)
XLA Ops:
  7.2 1.2 copy-done
  8.5 0.8 constant_dynamic-slice_fusion
  9.3 1.7 constant_dynamic-slice_fusion.1
  11.1 0.7 convert_element_type.79
  11.8 0.8 dynamic-slice_convert_fusion
  12.6 3.0 fusion.8
  15.6 31.2 %all-gather.15.cloned.1.call-done = bf16[5120,256]{1,0:T(8,128)(2,1)} async-done(((bf16[640,256]{1,0:T(8,128)(2,1)}), bf16[5120,256]{1,0:T(8,128)(2,1)}) %all-gather.15.cloned.1.call-update) | async-done | bytes 2621456 | tf_op jit(solution)/shard_map/all_gather | solution.py:114
  46.8 4.9 fusion.15
  51.8 0.5 all-gather.13.cloned.1.call-update
  52.5 0.8 dynamic-slice_convert_fusion.1
  54.1 27.9 %all-gather.9.cloned.1.call-done = bf16[5120,256]{1,0:T(8,128)(2,1)} async-done(((bf16[640,256]{1,0:T(8,128)(2,1)}), bf16[5120,256]{1,0:T(8,128)(2,1)}) %all-gather.9.cloned.1.call-update) | async-done | bytes 2621456 | tf_op jit(solution)/shard_map/all_gather | solution.py:113
  82.0 4.8 convolution_add_fusion.2
  86.8 0.7 pad_maximum_fusion.2
  87.6 0.5 all-gather.19.cloned.1.call-update
  88.7 2.2 compare_and_fusion
  90.9 17.5 %all-gather.17.cloned.1.call-done = bf16[3072,256]{1,0:T(8,128)(2,1)} async-done(((bf16[384,256]{1,0:T(8,128)(2,1)}), bf16[3072,256]{1,0:T(8,128)(2,1)}) %all-gather.17.cloned.1.call-update) | async-done | bytes 1572880 | tf_op jit(solution)/shard_map/all_gather | solution.py:158
  108.3 2.6 copy.47
  111.0 97.8 %all-gather.13.cloned.1.call-done = bf16[5120,1024]{1,0:T(8,128)(2,1)} async-done(((bf16[640,1024]{1,0:T(8,128)(2,1)}), bf16[5120,1024]{1,0:T(8,128)(2,1)}) %all-gather.13.cloned.1.call-update) | async-done | bytes 10485776 | tf_op jit(solution)/shard_map/all_gather | solution.py:112
  208.8 10.6 %convolution_add_fusion = f32[384,1024]{1,0:T(8,128)} fusion(bf16[5120,1024]{1,0:T(8,128)(2,1)} %all-gather.13.cloned.1.call-done, f32[1024]{0:T(1024)S(1)} %convert_element_type.84, bf16[384,5120]{1,0:T(8,128)(2,1)} %param.16, f32[5120]{0:T(1024)S(1)} %convert_element_type.79, f32[384]{0:T(512)S(1)} %add_rsqrt_fusion.1), kind=kOutput, calls=%fused_computation.38 | convolution fusion | flops 4034789376 | bytes 16016896 | tf_op jit(solution)/shard_map/dot_general | solution.py:125
  219.4 1.9 copy.33
  221.6 12.9 %all-gather.11.cloned.1.call-done = bf16[3072,256]{0,1:T(8,128)(2,1)} async-done(((bf16[384,256]{0,1:T(8,128)(2,1)}), bf16[3072,256]{0,1:T(8,128)(2,1)}) %all-gather.11.cloned.1.call-update) | async-done | bytes 1572880 | tf_op jit(solution)/shard_map/all_gather | solution.py:157
  234.5 17.0 %fusion = (f32[2,4,384]{2,1,0:T(4,128)S(1)}, f32[2,3072,384,4]{2,1,3,0:T(8,128)}) fusion(pred[384,3072]{0,1:T(8,128)(4,1)S(1)} %compare_and_fusion, bf16[3072,2,128,1]{0,2,3,1:T(8,128)(2,1)} %bitcast.75, bf16[384,2,4,128]{0,3,2,1:T(8,128)(2,1)S(1)} %bitcast.78), kind=kOutput, calls=%fused_computation.5 | convolution fusion | flops 2444227584 | bytes 41299968 | tf_op jit(solution)/shard_map/qgrd,kgd->grqk/dot_general | solution.py:166
  251.5 16.4 %fusion.3 = f32[2,4,384]{2,1,0:T(4,128)S(1)} fusion(f32[2,3072,384,4]{2,1,3,0:T(8,128)} %get-tuple-element.11, f32[2,4,384]{2,1,0:T(4,128)S(1)} %broadcast_maximum_fusion, pred[384,3072]{0,1:T(8,128)(4,1)S(1)} %compare_and_fusion), kind=kLoop, calls=%fused_computation.8 | loop fusion | flops 37745664 | bytes 38952960 | tf_op jit(solution)/shard_map/reduce_sum | solution.py:175
  267.9 16.4 %fusion.12 = bf16[384,2,4,128]{0,3,2,1:T(8,128)(2,1)} fusion(bf16[3072,2,128,1]{0,2,3,1:T(8,128)(2,1)S(1)} %bitcast.77, f32[2,3072,384,4]{2,1,3,0:T(8,128)} %get-tuple-element.11, f32[2,4,384]{2,1,0:T(4,128)S(1)} %broadcast_maximum_fusion, pred[384,3072]{0,1:T(8,128)(4,1)S(1)} %compare_and_fusion, f32[384,2,4]{0,2,1:T(4,128)S(1)} %bitcast.82), kind=kOutput, calls=%fused_computation.37 | convolution fusion | flops 2454454272 | bytes 41312256 | tf_op jit(solution)/shard_map/grqk,kgd->grqd/dot_general | solution.py:176
  284.3 50.2 %all-gather.19.cloned.1.call-done = bf16[1024,5120]{1,0:T(8,128)(2,1)} async-done(((bf16[1024,640]{1,0:T(8,128)(2,1)}), bf16[1024,5120]{1,0:T(8,128)(2,1)}) %all-gather.19.cloned.1.call-update) | async-done | bytes 10485776 | tf_op jit(solution)/shard_map/all_gather | solution.py:115
  334.5 10.5 %convolution_convert_fusion.1 = bf16[384,5120]{1,0:T(8,128)(2,1)} fusion(bf16[384,1024]{0,1:T(8,128)(2,1)} %bitcast.80, bf16[1024,5120]{1,0:T(8,128)(2,1)} %all-gather.19.cloned.1.call-done), kind=kOutput, calls=%fused_computation.22 | convolution fusion | flops 4028497920 | bytes 15204352 | tf_op jit(solution)/shard_map/dot_general | solution.py:208
  345.0 0.7 all-gather.21.cloned.1.call-update
  345.8 0.7 all-gather.23.cloned.1.call-update
  346.8 28.2 %collective-permute-done = bf16[1728,640]{1,0:T(8,128)(2,1)S(1)} collective-permute-done((bf16[1728,640]{1,0:T(8,128)(2,1)S(1)}, bf16[1728,640]{1,0:T(8,128)(2,1)S(1)}, u32[]{:S(2)}, u32[]{:S(2)}) %collective-permute-start) | collective-permute-done | bytes 2211872 | tf_op jit(solution)/shard_map/ppermute | solution.py:28
  375.1 3.5 collective-permute-start.4
  378.6 45.9 %collective-permute-done.1 = bf16[1728,640]{1,0:T(8,128)(2,1)S(1)} collective-permute-done((bf16[1728,640]{1,0:T(8,128)(2,1)S(1)}, bf16[1728,640]{1,0:T(8,128)(2,1)S(1)}, u32[]{:S(2)}, u32[]{:S(2)}) %collective-permute-start.1) | collective-permute-done | bytes 2211872 | tf_op jit(solution)/shard_map/ppermute | solution.py:28
  424.5 3.5 collective-permute-start.5
  428.1 62.2 %collective-permute-done.2 = bf16[1728,640]{1,0:T(8,128)(2,1)} collective-permute-done((bf16[1728,640]{1,0:T(8,128)(2,1)S(1)}, bf16[1728,640]{1,0:T(8,128)(2,1)}, u32[]{:S(2)}, u32[]{:S(2)}) %collective-permute-start.2) | collective-permute-done | bytes 2211872 | tf_op jit(solution)/shard_map/ppermute | solution.py:28
  490.3 6.5 collective-permute-done.5
  496.8 3.7 collective-permute-start.6
  500.5 88.4 %collective-permute-done.3 = bf16[1728,640]{1,0:T(8,128)(2,1)} collective-permute-done((bf16[1728,640]{1,0:T(8,128)(2,1)}, bf16[1728,640]{1,0:T(8,128)(2,1)}, u32[]{:S(2)}, u32[]{:S(2)}) %collective-permute-start.3) | collective-permute-done | bytes 2211872 | tf_op jit(solution)/shard_map/ppermute | solution.py:28
  588.9 3.3 bitcast_dynamic-update-slice_fusion.7
  592.2 3.2 bitcast_dynamic-update-slice_fusion.6
  595.4 1.6 bitcast_dynamic-update-slice_fusion.5
  596.9 1.6 bitcast_dynamic-update-slice_fusion.4
  598.5 1.5 bitcast_dynamic-update-slice_fusion.3
  600.1 3.2 bitcast_dynamic-update-slice_fusion.2
  603.3 3.2 bitcast_dynamic-update-slice_fusion.1
  606.5 1.5 bitcast_dynamic-update-slice_fusion
  608.1 8.3 mini-gather-slice.2
  616.4 7.4 mini-gather-slice.3
  623.8 9.2 %gather_fusion.1 = bf16[8,896,640]{2,1,0:T(8,128)(2,1)} fusion(bf16[8,896,640]{2,1,0:T(8,128)(2,1)} %mini-gather-slice.2, s32[1024]{0:T(1024)S(1)} %pad_clamp_fusion.1), kind=kCustom, calls=%fused_computation.1 | custom fusion | bytes 18350112 | tf_op jit(solution)/shard_map/gather | solution.py:33
  632.9 8.5 gather_fusion.2
  641.4 8.2 maximum_bitcast_fusion
  649.6 7.6 copy.48
  657.2 7.8 convert_add_fusion
  665.0 2.1 all-gather.21.cloned.1.call-done
  667.1 16.5 %fusion.38 = f32[384,1728]{0,1:T(8,128)} fusion(bf16[5120,1728]{0,1:T(8,128)(2,1)} %all-gather.21.cloned.1.call-done, f32[5120]{0:T(1024)S(1)} %convert_element_type.93, f32[384]{0:T(512)S(1)} %add_rsqrt_fusion, bf16[384,5120]{1,0:T(8,128)(2,1)} %param.16, bf16[384,5120]{1,0:T(8,128)(2,1)} %all-reduce.2.cloned.1.call-done), kind=kOutput, calls=%fused_computation.114 | convolution fusion | flops 6806568960 | bytes 28235264 | tf_op jit(solution)/shard_map/dot_general | solution.py:212
  683.6 141.9 %all-gather.23.cloned.1.call-done = bf16[5120,1728]{0,1:T(8,128)(2,1)} async-done(((bf16[640,1728]{0,1:T(8,128)(2,1)}), bf16[5120,1728]{0,1:T(8,128)(2,1)}) %all-gather.23.cloned.1.call-update) | async-done | bytes 17694736 | tf_op jit(solution)/shard_map/all_gather | solution.py:117
  825.5 28.2 %convolution_convert_fusion = bf16[384,5120]{1,0:T(8,128)(2,1)} fusion(bf16[1728,5120]{1,0:T(8,128)(2,1)} %bitcast.73, bf16[5120,1728]{0,1:T(8,128)(2,1)} %all-gather.23.cloned.1.call-done, f32[384,1728]{0,1:T(8,128)} %fusion.38, f32[5120]{0:T(1024)S(1)} %convert_element_type.93, f32[384]{0:T(512)S(1)} %add_rsqrt_fusion, bf16[384,5120]{1,0:T(8,128)(2,1)} %param.16, ...), kind=kOutput, calls=%fused_computation.21 | convolution fusion | flops 13607288832 | bytes 49862144 | tf_op jit(solution)/shard_map/dot_general | solution.py:217
  854.6 5.0 copy.39
  859.7 1.9 stack_reshape.7
  861.5 6.4 pad_maximum_fusion
  867.9 13.4 %copy.40 = bf16[3072,2,2,128]{3,2,1,0:T(2,128)(2,1)} copy(bf16[3072,2,2,128]{3,1,0,2:T(2,128)(2,1)S(1)} %pad_maximum_fusion) | data formatting | bytes 6291456 | tf_op jit(solution)/shard_map/stack | solution.py:187
  881.3 5.7 reshape.381
  887.0 4.8 gather_fusion
  891.8 0.9 select_select_fusion
  892.7 9.9 %reduce-scatter.2.cloned.1.call-done = bf16[96,5120]{1,0:T(8,128)(2,1)} async-done(((bf16[384,5120]{1,0:T(8,128)(2,1)}), bf16[96,5120]{1,0:T(8,128)(2,1)}) %reduce-scatter.2.cloned.1.call-update) | async-done | bytes 983056 | tf_op jit(solution)/shard_map/reduce_scatter | solution.py:216
  902.6 3.0 add_convert_fusion
  (88 shorter events, 3.6 us)
Async XLA Ops:
  7.2 1.3 copy-start
  7.2 39.7 %all-gather.15.cloned.1.call-start = ((), (), s32[]{:S(2)}) async-start(), calls=%async_computation.4 | async-start | bytes 2949120 | tf_op jit(solution)/shard_map/all_gather | solution.py:114
  9.3 72.7 %all-gather.9.cloned.1.call-start = ((), (), s32[]{:S(2)}) async-start(), calls=%async_computation.1 | async-start | bytes 2949120 | tf_op jit(solution)/shard_map/all_gather | solution.py:113
  11.1 97.3 %all-gather.17.cloned.1.call-start = ((), (), s32[]{:S(2)}) async-start(), calls=%async_computation.5 | async-start | bytes 1769472 | tf_op jit(solution)/shard_map/all_gather | solution.py:158
  12.6 39.8 %copy-start.13 = (s32[4]{0:T(128)S(1)}, s32[4]{0:T(128)}, u32[]{:S(2)}) copy-start(s32[4]{0:T(128)} %param.29) | copy-start | bytes 52
  12.6 40.7 %copy-start.11 = (s32[16]{0:T(128)S(1)}, s32[16]{0:T(128)}, u32[]{:S(2)}) copy-start(s32[16]{0:T(128)} %param.30) | copy-start | bytes 196
  51.7 157.1 %all-gather.13.cloned.1.call-start = ((), (), s32[]{:S(2)}) async-start(), calls=%async_computation.3 | async-start | bytes 11796480 | tf_op jit(solution)/shard_map/all_gather | solution.py:112
  52.3 182.2 %all-gather.11.cloned.1.call-start = ((), (), s32[]{:S(2)}) async-start(), calls=%async_computation.2 | async-start | bytes 1769472 | tf_op jit(solution)/shard_map/all_gather | solution.py:157
  54.1 34.4 %copy-start.10 = (bf16[1024]{0:T(1024)(128)(2,1)S(1)}, bf16[1024]{0:T(1024)(128)(2,1)}, u32[]{:S(2)}) copy-start(bf16[1024]{0:T(1024)(128)(2,1)} %param.26) | copy-start | bytes 6148
  87.5 247.0 %all-gather.19.cloned.1.call-start = ((), (), s32[]{:S(2)}) async-start(), calls=%async_computation.6 | async-start | bytes 11796480 | tf_op jit(solution)/shard_map/all_gather | solution.py:115
  88.1 569.2 %all-reduce.2.cloned.1.call-start = ((), (), s32[]{:S(2)}) async-start(), calls=%async_computation.7 | async-start | bytes 7864320 | tf_op jit(solution)/shard_map/psum | solution.py:207
  251.5 16.4 %copy-start.8 = (bf16[3072,256]{0,1:T(8,128)(2,1)S(1)}, bf16[3072,256]{0,1:T(8,128)(2,1)}, u32[]{:S(2)}) copy-start(bf16[3072,256]{0,1:T(8,128)(2,1)} %copy.47) | copy-start | bytes 4718596
  345.0 1.6 copy-start.3
  345.0 145.3 %copy-start.9 = (bf16[5120]{0:T(1024)(128)(2,1)S(1)}, bf16[5120]{0:T(1024)(128)(2,1)}, u32[]{:S(2)}) copy-start(bf16[5120]{0:T(1024)(128)(2,1)} %param.18) | copy-start | bytes 30724
  345.0 322.1 %all-gather.21.cloned.1.call-start = ((), (), s32[]{:S(2)}) async-start(), calls=%async_computation.8 | async-start | bytes 19906560 | tf_op jit(solution)/shard_map/all_gather | solution.py:116
  345.7 479.8 %all-gather.23.cloned.1.call-start = ((), (), s32[]{:S(2)}) async-start(), calls=%async_computation.9 | async-start | bytes 19906560 | tf_op jit(solution)/shard_map/all_gather | solution.py:117
  346.5 556.2 %reduce-scatter.2.cloned.1.call-start = ((), (), s32[]{:S(2)}) async-start(), calls=%async_computation.10 | async-start | bytes 4915200 | tf_op jit(solution)/shard_map/reduce_scatter | solution.py:216
  346.6 28.5 %collective-permute-start = (bf16[1728,640]{1,0:T(8,128)(2,1)S(1)}, bf16[1728,640]{1,0:T(8,128)(2,1)S(1)}, u32[]{:S(2)}, u32[]{:S(2)}) collective-permute-start(bf16[1728,640]{1,0:T(8,128)(2,1)S(1)} %copy-done.3), channel_id=1, source_target_pairs={{0,4},{4,8},{8,12},{12,16},{16,20},{20,24},{24,28},{28,0},{1,5},{5... | collective-permute-start | bytes 6635528 | tf_op jit(solution)/shard_map/ppermute | solution.py:28
  375.1 49.4 %copy-start.4 = (bf16[1728,640]{1,0:T(8,128)(2,1)}, bf16[1728,640]{1,0:T(8,128)(2,1)S(1)}, u32[]{:S(2)}) copy-start(bf16[1728,640]{1,0:T(8,128)(2,1)S(1)} %collective-permute-done) | copy-start | bytes 6635524
  375.1 49.4 %collective-permute-start.1 = (bf16[1728,640]{1,0:T(8,128)(2,1)S(1)}, bf16[1728,640]{1,0:T(8,128)(2,1)S(1)}, u32[]{:S(2)}, u32[]{:S(2)}) collective-permute-start(bf16[1728,640]{1,0:T(8,128)(2,1)S(1)} %collective-permute-done), channel_id=1, source_target_pairs={{0,4},{4,8},{8,12},{12,16},{16,20},{20,24},{24,28},{28,0},{1,5},{5... | collective-permute-start | bytes 6635528 | tf_op jit(solution)/shard_map/ppermute | solution.py:28
  375.1 49.4 %collective-permute-start.4 = (bf16[1728,640]{1,0:T(8,128)(2,1)S(1)}, bf16[1728,640]{1,0:T(8,128)(2,1)}, u32[]{:S(2)}, u32[]{:S(2)}) collective-permute-start(bf16[1728,640]{1,0:T(8,128)(2,1)S(1)} %copy-done.3), channel_id=1, source_target_pairs={{4,0},{8,4},{12,8},{16,12},{20,16},{24,20},{28,24},{0,28},{5,1},{9... | collective-permute-start | bytes 6635528 | tf_op jit(solution)/shard_map/ppermute | solution.py:30
  424.5 3.6 copy-start.6
  424.5 65.8 %collective-permute-start.2 = (bf16[1728,640]{1,0:T(8,128)(2,1)S(1)}, bf16[1728,640]{1,0:T(8,128)(2,1)}, u32[]{:S(2)}, u32[]{:S(2)}) collective-permute-start(bf16[1728,640]{1,0:T(8,128)(2,1)S(1)} %collective-permute-done.1), channel_id=1, source_target_pairs={{0,4},{4,8},{8,12},{12,16},{16,20},{20,24},{24,28},{28,0},{1,5},{5... | collective-permute-start | bytes 6635528 | tf_op jit(solution)/shard_map/ppermute | solution.py:28
  424.5 72.3 %collective-permute-start.5 = (bf16[1728,640]{1,0:T(8,128)(2,1)}, bf16[1728,640]{1,0:T(8,128)(2,1)}, u32[]{:S(2)}, u32[]{:S(2)}) collective-permute-start(bf16[1728,640]{1,0:T(8,128)(2,1)} %collective-permute-done.4), channel_id=1, source_target_pairs={{4,0},{8,4},{12,8},{16,12},{20,16},{24,20},{28,24},{0,28},{5,1},{9... | collective-permute-start | bytes 6635528 | tf_op jit(solution)/shard_map/ppermute | solution.py:30
  490.3 98.7 %collective-permute-start.3 = (bf16[1728,640]{1,0:T(8,128)(2,1)}, bf16[1728,640]{1,0:T(8,128)(2,1)}, u32[]{:S(2)}, u32[]{:S(2)}) collective-permute-start(bf16[1728,640]{1,0:T(8,128)(2,1)} %collective-permute-done.2), channel_id=1, source_target_pairs={{0,4},{4,8},{8,12},{12,16},{16,20},{20,24},{24,28},{28,0},{1,5},{5... | collective-permute-start | bytes 6635528 | tf_op jit(solution)/shard_map/ppermute | solution.py:28
  490.3 105.1 %copy-start.7 = (bf16[1728,640]{1,0:T(8,128)(2,1)S(1)}, bf16[1728,640]{1,0:T(8,128)(2,1)}, u32[]{:S(2)}) copy-start(bf16[1728,640]{1,0:T(8,128)(2,1)} %copy-done.6) | copy-start | bytes 6635524
  490.3 106.6 %copy-start.5 = (bf16[1728,640]{1,0:T(8,128)(2,1)S(1)}, bf16[1728,640]{1,0:T(8,128)(2,1)}, u32[]{:S(2)}) copy-start(bf16[1728,640]{1,0:T(8,128)(2,1)} %copy-done.4) | copy-start | bytes 6635524
  496.8 109.7 %collective-permute-start.6 = (bf16[1728,640]{1,0:T(8,128)(2,1)}, bf16[1728,640]{1,0:T(8,128)(2,1)S(1)}, u32[]{:S(2)}, u32[]{:S(2)}) collective-permute-start(bf16[1728,640]{1,0:T(8,128)(2,1)} %collective-permute-done.5), channel_id=1, source_target_pairs={{4,0},{8,4},{12,8},{16,12},{20,16},{24,20},{28,24},{0,28},{5,1},{9... | collective-permute-start | bytes 6635528 | tf_op jit(solution)/shard_map/ppermute | solution.py:30
  825.5 28.3 %copy-start.14 = (s32[16]{0:T(128)S(1)}, s32[16]{0:T(128)}, u32[]{:S(2)}) copy-start(s32[16]{0:T(128)} %param.31) | copy-start | bytes 196
  825.5 28.5 %copy-start.12 = (s32[16]{0:T(128)S(1)}, s32[16]{0:T(128)}, u32[]{:S(2)}) copy-start(s32[16]{0:T(128)} %param.30) | copy-start | bytes 196
  853.7 5.9 copy-start.2
  867.9 37.7 %copy-start.1 = (bf16[640,1024]{1,0:T(8,128)(2,1)S(1)}, bf16[640,1024]{1,0:T(8,128)(2,1)}, u32[]{:S(2)}) copy-start(bf16[640,1024]{1,0:T(8,128)(2,1)} %param.21) | copy-start | bytes 3932164
Sparse Core Ops, SparseCore 0:
  10.2 36.5 all-gather.14
  49.1 32.8 all-gather.8
  84.2 24.1 all-gather.16
  109.8 98.9 all-gather.12
  210.8 23.5 all-gather.10
  235.9 98.5 all-gather.18
  345.1 98.7 all-reduce.1
  445.6 221.4 all-gather.20
  668.8 156.6 all-gather.22
  853.9 48.7 reduce-scatter.1
